TPU v7x, 128 devices: a whole 4x4x4 slice. The times are simulated.
128 devices in a mesh: row: 8 (over x_lo, z), col: 16 (over y, x_hi, core).
Axes of the slice: x: 4 (x_hi: 2, x_lo: 2; x = x_hi * 2 + x_lo), y: 4, z: 4, core: 2. Of those that a mesh axis runs over, the one named last changes fastest.
Arguments:
- tokens: bfloat16 [1024, 12288], P('col', 'row'), may hold values from -6 to 6
- up_weight: bfloat16 [12288, 24576], P('row', 'col'), may hold values from -0.109375 to 0.109375
- up_mask: int32 [192, 384], P('row', 'col'), may hold values 0 or 1
- down_weight: bfloat16 [24576, 12288], P('col', 'row'), may hold values from -0.078125 to 0.078125
- down_mask: int32 [384, 192], P('col', 'row'), may hold values 0 or 1
- grad_out: bfloat16 [1024, 12288], P('col', 'row'), may hold values from -6 to 6
Outputs:
- out_heads: bfloat16 [96, 1024, 128], P('row', 'col')
- grad_tokens: bfloat16 [1024, 12288], P('col', 'row')
- grad_up: bfloat16 [12288, 24576], P('row', 'col')
- grad_down: bfloat16 [24576, 12288], P('col', 'row')
All inputs are finite; a program needn't handle non-finite values. No bound on the sum of `up_mask` or of `down_mask` on one device may be relied on, other than what follows from the above.
Results may differ from a plain program's by a relative error of at most 0.022.
Values may be sent and summed in bfloat16 or wider, within the bound.
A program may use at most 192 MiB of HBM per device.

v0:
```python
import math
import jax
import jax.numpy as jnp
from jax import lax
from jax.sharding import PartitionSpec as P

BLOCK = 64
HEAD_DIM = 128


def expand(weight, mask):
    rows_in, cols_in = weight.shape
    tiles = weight.reshape(rows_in // BLOCK, BLOCK, cols_in // BLOCK, BLOCK)
    tiles = tiles * mask.astype(weight.dtype)[:, None, :, None]
    return tiles.reshape(rows_in, cols_in)


def activate(value):
    return jax.nn.gelu(value, approximate=True)


def times_transposed(left, right):
    return lax.dot_general(
        left, right, (((1,), (1,)), ((), ())), preferred_element_type=jnp.float32
    )


def over_tokens(left, right):
    return lax.dot_general(
        left, right, (((0,), (0,)), ((), ())), preferred_element_type=jnp.float32
    )


def body(tokens, up_weight, up_mask, down_weight, down_mask, grad_out):
    w_up = expand(up_weight, up_mask)
    w_down = expand(down_weight, down_mask)
    tok_all = lax.all_gather(tokens, "col", axis=0, tiled=True)
    token_count = tok_all.shape[0]
    col_share = token_count // lax.axis_size("col")
    piece = tok_all
    pre_act = lax.psum_scatter(
        jnp.dot(piece, w_up, preferred_element_type=jnp.float32).astype(jnp.bfloat16),
        "row",
        scatter_dimension=0,
        tiled=True,
    ).astype(jnp.float32)
    hidden = activate(pre_act).astype(jnp.bfloat16)
    hidden_all = lax.all_gather(hidden, "row", axis=0, tiled=True)
    piece = hidden_all
    output_rows = lax.psum_scatter(
        jnp.dot(piece, w_down, preferred_element_type=jnp.float32).astype(jnp.bfloat16),
        "col",
        scatter_dimension=0,
        tiled=True,
    )
    out_heads = output_rows.reshape(
        col_share, output_rows.shape[1] // HEAD_DIM, HEAD_DIM
    ).transpose(1, 0, 2)
    cot_all = lax.all_gather(grad_out, "col", axis=0, tiled=True)
    piece = cot_all
    grad_hidden = lax.psum_scatter(
        times_transposed(piece, w_down).astype(jnp.bfloat16), "row", scatter_dimension=0, tiled=True
    ).astype(jnp.float32)
    unused, pull = jax.vjp(activate, pre_act)
    grad_pre = pull(grad_hidden)[0].astype(jnp.bfloat16)
    grad_pre_all = lax.all_gather(grad_pre, "row", axis=0, tiled=True)
    grad_scale = 1.0 / math.sqrt(token_count)
    grad_up = expand(over_tokens(tok_all, grad_pre_all) * grad_scale, up_mask).astype(jnp.bfloat16)
    grad_down = expand(over_tokens(hidden_all, cot_all) * grad_scale, down_mask).astype(
        jnp.bfloat16
    )
    piece = grad_pre_all
    grad_tokens = lax.psum_scatter(
        times_transposed(piece, w_up).astype(jnp.bfloat16), "col", scatter_dimension=0, tiled=True
    )
    return (out_heads, grad_tokens, grad_up, grad_down)


def solution(mesh):
    return jax.shard_map(
        body,
        mesh=mesh,
        in_specs=(
            P("col", "row"),
            P("row", "col"),
            P("row", "col"),
            P("col", "row"),
            P("col", "row"),
            P("col", "row"),
        ),
        out_specs=(P("row", "col", None), P("col", "row"), P("row", "col"), P("col", "row")),
        check_vma=False,
    )
```

profile of v0, /device:TPU:0, one launch (start us, length us, event | category | flops | bytes accessed | tf_op | source)
XLA Modules:
  0.0 489.4 jit_solution(12928435325429374456)
XLA Ops:
  7.2 0.0 all-gather.9.cloned.1.call-start
  7.2 0.7 all-gather.9.cloned.1.call-update
  7.9 0.0 all-gather.5.cloned.1.call-start
  7.9 0.7 all-gather.5.cloned.1.call-update
  8.6 0.0 reduce-scatter.15.cloned.1.call-start
  8.7 0.8 fusion.18
  9.5 4.9 %mul.107 = bf16[24,64,24,64]{3,2,1,0:T(8,128)(2,1)} broadcast(bf16[24,24]{1,0:T(8,128)(2,1)S(1)} %get-tuple-element.19), dimensions={0,2} | broadcast | bytes 4719744 | tf_op jit(solution)/shard_map/mul | solution.py:14
  14.4 13.1 %mul.108 = bf16[1536,1536]{1,0:T(8,128)(2,1)} reshape(bf16[24,64,24,64]{3,2,1,0:T(8,128)(2,1)} %mul.107) | data formatting | bytes 9437184 | tf_op jit(solution)/shard_map/mul | solution.py:14
  27.5 35.9 %all-gather.9.cloned.1.call-done = bf16[1024,1536]{1,0:T(8,128)(2,1)} async-done(((bf16[64,1536]{1,0:T(8,128)(2,1)}), bf16[1024,1536]{1,0:T(8,128)(2,1)}) %all-gather.9.cloned.1.call-update) | async-done | bytes 3145744 | tf_op jit(solution)/shard_map/all_gather | solution.py:59
  63.4 9.5 %fusion.4 = bf16[1024,1536]{0,1:T(8,128)(2,1)S(1)} fusion(bf16[1024,1536]{1,0:T(8,128)(2,1)} %all-gather.9.cloned.1.call-done, bf16[1536,1536]{1,0:T(8,128)(2,1)} %param.9, bf16[1536,1536]{1,0:T(8,128)(2,1)} %mul.108), kind=kOutput, calls=%fused_computation.11 | convolution fusion | flops 4835770368 | bytes 15728640 | tf_op jit(solution)/shard_map/dot_general | solution.py:23
  72.9 0.0 copy-start
  73.0 2.9 copy.21
  75.9 0.0 reduce-scatter.15.cloned.1.call-update
  75.9 0.2 reduce-scatter.13.cloned.1.call-start
  76.1 0.0 copy-done
  76.2 4.9 %mul.100 = bf16[24,64,24,64]{3,2,1,0:T(8,128)(2,1)} broadcast(bf16[24,24]{1,0:T(8,128)(2,1)S(1)} %get-tuple-element.21), dimensions={0,2} | broadcast | bytes 4719744 | tf_op jit(solution)/shard_map/mul | solution.py:14
  81.1 13.0 %mul.101 = bf16[1536,1536]{1,0:T(8,128)(2,1)} reshape(bf16[24,64,24,64]{3,2,1,0:T(8,128)(2,1)} %mul.100) | data formatting | bytes 9437184 | tf_op jit(solution)/shard_map/mul | solution.py:14
  94.2 7.6 %mul.102 = bf16[1536,1536]{1,0:T(8,128)(2,1)} multiply(bf16[1536,1536]{1,0:T(8,128)(2,1)} %param.7, bf16[1536,1536]{1,0:T(8,128)(2,1)} %mul.101) | non-fusion elementwise | flops 2359296 | bytes 14155776 | tf_op jit(solution)/shard_map/mul | solution.py:14
  101.8 13.4 %all-gather.5.cloned.1.call-done = bf16[1024,1536]{1,0:T(8,128)(2,1)} async-done(((bf16[64,1536]{1,0:T(8,128)(2,1)}), bf16[1024,1536]{1,0:T(8,128)(2,1)}) %all-gather.5.cloned.1.call-update) | async-done | bytes 3145744 | tf_op jit(solution)/shard_map/all_gather | solution.py:37
  115.2 8.2 %fusion.3 = bf16[1024,1536]{0,1:T(8,128)(2,1)S(1)} fusion(bf16[1536,1536]{1,0:T(8,128)(2,1)} %mul.102, bf16[1024,1536]{1,0:T(8,128)(2,1)} %all-gather.5.cloned.1.call-done), kind=kOutput, calls=%fused_computation.10 | convolution fusion | flops 4833411072 | bytes 11010048 | tf_op jit(solution)/shard_map/dot_general | solution.py:42
  123.4 3.0 copy.19
  126.3 0.0 reduce-scatter.13.cloned.1.call-update
  126.3 0.0 all-gather.7.cloned.1.call-start
  126.4 36.6 %reduce-scatter.15.cloned.1.call-done = bf16[128,1536]{1,0:T(8,128)(2,1)} async-done(((bf16[1024,1536]{1,0:T(8,128)(2,1)}), bf16[128,1536]{1,0:T(8,128)(2,1)}) %reduce-scatter.15.cloned.1.call-update) | async-done | bytes 393232
  163.0 1.2 copy.22
  164.3 47.4 %reduce-scatter.13.cloned.1.call-done = bf16[128,1536]{1,0:T(8,128)(2,1)} async-done(((bf16[1024,1536]{1,0:T(8,128)(2,1)}), bf16[128,1536]{1,0:T(8,128)(2,1)}) %reduce-scatter.13.cloned.1.call-update) | async-done | bytes 393232
  211.7 1.2 copy.20
  212.9 1.5 fusion.10
  214.4 0.0 all-gather.7.cloned.1.call-update
  214.5 0.0 all-gather.11.cloned.1.call-start
  214.5 0.5 all-gather.11.cloned.1.call-update
  215.0 0.0 reduce-scatter.9.cloned.1.call-start
  215.1 51.8 %all-gather.7.cloned.1.call-done = bf16[1024,1536]{0,1:T(8,128)(2,1)} async-done(((bf16[128,1536]{0,1:T(8,128)(2,1)}), bf16[1024,1536]{0,1:T(8,128)(2,1)}) %all-gather.7.cloned.1.call-update) | async-done | bytes 3145744 | tf_op jit(solution)/shard_map/all_gather | solution.py:48
  266.9 10.7 %convolution_convert_fusion.2 = bf16[1024,1536]{1,0:T(8,128)(2,1)} fusion(bf16[1024,1536]{0,1:T(8,128)(2,1)} %all-gather.7.cloned.1.call-done, bf16[1536,1536]{1,0:T(8,128)(2,1)} %param.9, bf16[1536,1536]{1,0:T(8,128)(2,1)} %mul.108), kind=kOutput, calls=%fused_computation.8 | convolution fusion | flops 4835770368 | bytes 15728640 | tf_op jit(solution)/shard_map/dot_general | solution.py:51
  277.6 0.0 reduce-scatter.9.cloned.1.call-update
  277.6 0.3 reduce-scatter.11.cloned.1.call-start
  277.9 45.0 %all-gather.11.cloned.1.call-done = bf16[1024,1536]{0,1:T(8,128)(2,1)} async-done(((bf16[128,1536]{0,1:T(8,128)(2,1)}), bf16[1024,1536]{0,1:T(8,128)(2,1)}) %all-gather.11.cloned.1.call-update) | async-done | bytes 3145744 | tf_op jit(solution)/shard_map/all_gather | solution.py:66
  322.8 9.3 %convolution_convert_fusion = bf16[1024,1536]{1,0:T(8,128)(2,1)} fusion(bf16[1024,1536]{0,1:T(8,128)(2,1)} %all-gather.11.cloned.1.call-done, bf16[1536,1536]{1,0:T(8,128)(2,1)} %mul.102), kind=kOutput, calls=%fused_computation.6 | convolution fusion | flops 4833411072 | bytes 11010048 | tf_op jit(solution)/shard_map/dot_general | solution.py:23
  332.1 0.0 reduce-scatter.11.cloned.1.call-update
  332.1 0.1 copy.16
  332.2 8.1 %mul.127 = f32[24,64,24,64]{3,2,1,0:T(8,128)} broadcast(f32[24,24]{1,0:T(8,128)S(1)} %get-tuple-element.18), dimensions={0,2} | broadcast | bytes 9439488 | tf_op jit(solution)/shard_map/mul | solution.py:14
  340.3 16.6 %mul.128 = f32[1536,1536]{1,0:T(8,128)} reshape(f32[24,64,24,64]{3,2,1,0:T(8,128)} %mul.127) | data formatting | bytes 18874368 | tf_op jit(solution)/shard_map/mul | solution.py:14
  356.9 7.9 %mul.123 = f32[24,64,24,64]{1,0,3,2:T(8,128)} broadcast(f32[24,24]{0,1:T(8,128)S(1)} %copy.16), dimensions={0,2} | broadcast | bytes 9439488 | tf_op jit(solution)/shard_map/mul | solution.py:14
  364.8 0.0 copy-start.2
  364.8 16.5 %mul.124 = f32[1536,1536]{0,1:T(8,128)} reshape(f32[24,64,24,64]{1,0,3,2:T(8,128)} %mul.123) | data formatting | bytes 18874368 | tf_op jit(solution)/shard_map/mul | solution.py:14
  381.4 0.0 copy-done.2
  381.4 10.0 %fusion.1 = bf16[1536,1536]{0,1:T(8,128)(2,1)} fusion(f32[1536,1536]{0,1:T(8,128)} %mul.124, bf16[1024,1536]{0,1:T(8,128)(2,1)} %all-gather.11.cloned.1.call-done, bf16[1024,1536]{1,0:T(8,128)(2,1)S(1)} %copy-done.2), kind=kOutput, calls=%fused_computation.4 | convolution fusion | flops 4838916096 | bytes 20447232 | tf_op jit(solution)/shard_map/dot_general | solution.py:29
  391.4 0.0 copy-start.1
  391.4 6.8 %copy.18 = bf16[1536,1536]{1,0:T(8,128)(2,1)} copy(bf16[1536,1536]{0,1:T(8,128)(2,1)} %fusion.1) | data formatting | bytes 9437184
  398.2 0.0 copy-done.1
  398.2 10.1 %fusion.2 = bf16[1536,1536]{1,0:T(8,128)(2,1)} fusion(f32[1536,1536]{1,0:T(8,128)} %mul.128, bf16[1024,1536]{0,1:T(8,128)(2,1)} %all-gather.7.cloned.1.call-done, bf16[1024,1536]{1,0:T(8,128)(2,1)S(1)} %copy-done.1), kind=kOutput, calls=%fused_computation.5 | convolution fusion | flops 4838916096 | bytes 20447232 | tf_op jit(solution)/shard_map/dot_general | solution.py:29
  408.3 0.0 reduce-scatter.9.cloned.1.call-done
  408.3 1.1 reshape.27
  409.4 0.7 copy.17
  410.1 72.4 %reduce-scatter.11.cloned.1.call-done = bf16[64,1536]{1,0:T(8,128)(2,1)} async-done(((bf16[1024,1536]{1,0:T(8,128)(2,1)}), bf16[64,1536]{1,0:T(8,128)(2,1)}) %reduce-scatter.11.cloned.1.call-update) | async-done | bytes 196624 | tf_op jit(solution)/shard_map/reduce_scatter | solution.py:73
  (1 shorter events, 0.0 us)
Async XLA Ops:
  7.2 56.2 %all-gather.9.cloned.1.call-start = ((), (), s32[]{:S(2)}) async-start(), calls=%async_computation.7 | async-start | bytes 3342336 | tf_op jit(solution)/shard_map/all_gather | solution.py:59
  7.9 107.3 %all-gather.5.cloned.1.call-start = ((), (), s32[]{:S(2)}) async-start(), calls=%async_computation.4 | async-start | bytes 3342336 | tf_op jit(solution)/shard_map/all_gather | solution.py:37
  8.6 154.4 %reduce-scatter.15.cloned.1.call-start = ((), (), s32[]{:S(2)}) async-start(), calls=%async_computation.11 | async-start | bytes 3538944
  72.9 3.2 copy-start
  75.9 135.8 %reduce-scatter.13.cloned.1.call-start = ((), (), s32[]{:S(2)}) async-start(), calls=%async_computation.10 | async-start | bytes 3538944
  126.3 140.5 %all-gather.7.cloned.1.call-start = ((), (), s32[]{:S(2)}) async-start(), calls=%async_computation.5 | async-start | bytes 3538944 | tf_op jit(solution)/shard_map/all_gather | solution.py:48
  214.5 108.4 %all-gather.11.cloned.1.call-start = ((), (), s32[]{:S(2)}) async-start(), calls=%async_computation.8 | async-start | bytes 3538944 | tf_op jit(solution)/shard_map/all_gather | solution.py:66
  215.0 193.3 %reduce-scatter.9.cloned.1.call-start = ((), (), s32[]{:S(2)}) async-start(), calls=%async_computation.6 | async-start | bytes 3342336 | tf_op jit(solution)/shard_map/reduce_scatter | solution.py:50
  277.6 205.0 %reduce-scatter.11.cloned.1.call-start = ((), (), s32[]{:S(2)}) async-start(), calls=%async_computation.9 | async-start | bytes 3342336 | tf_op jit(solution)/shard_map/reduce_scatter | solution.py:73
  364.8 16.6 %copy-start.2 = (bf16[1024,1536]{1,0:T(8,128)(2,1)S(1)}, bf16[1024,1536]{1,0:T(8,128)(2,1)}, u32[]{:S(2)}) copy-start(bf16[1024,1536]{1,0:T(8,128)(2,1)} %all-gather.5.cloned.1.call-done) | copy-start | bytes 9437188
  391.4 6.8 %copy-start.1 = (bf16[1024,1536]{1,0:T(8,128)(2,1)S(1)}, bf16[1024,1536]{1,0:T(8,128)(2,1)}, u32[]{:S(2)}) copy-start(bf16[1024,1536]{1,0:T(8,128)(2,1)} %all-gather.9.cloned.1.call-done) | copy-start | bytes 9437188
Sparse Core Ops, SparseCore 0:
  10.4 52.9 all-gather.8
  65.9 49.2 all-gather.4
  117.6 45.3 reduce-scatter.14
  165.3 46.3 reduce-scatter.12
  214.6 52.2 all-gather.6
  268.3 54.4 all-gather.10
  326.9 76.7 reduce-scatter.8
  408.3 74.1 reduce-scatter.10
where the time goes:
time: 491 us; the launch traced here: 489 us
  waiting for transfers between devices  305 us (62%)
  local copies, waits for them, and re-layouts  102 us (21%)
  matrix products  57.8 us (12%)
  between operations  14.2 us (3%)
  other arithmetic  9.97 us (2%)
    unnamed x10, waiting for transfers between devices  86 us
    mul x8, local copies, waits for them, and re-layouts, expand(): tiles = tiles * mask.astype(weight.dtype)[:, None, :, None]  85.2 us
    reduce_scatter x1, waiting for transfers between devices, body(): lax.psum_scatter(times_transposed(piece, w_up).astype(jnp.bfloat16), 'col...  72.4 us
    all_gather x1, waiting for transfers between devices, body(): hidden_all = lax.all_gather(hidden, 'row', axis=0, tiled=True)  51.8 us
    all_gather x1, waiting for transfers between devices, body(): grad_pre_all = lax.all_gather(grad_pre, 'row', axis=0, tiled=True)  45 us
    all_gather x1, waiting for transfers between devices, body(): cot_all = lax.all_gather(grad_out, 'col', axis=0, tiled=True)  35.9 us
    dot_general x2, matrix products, over_tokens(): lax.dot_general(left, right, (((0,), (0,)), ((), ())), preferred_element_...  20.1 us
    dot_general x2, matrix products, times_transposed(): lax.dot_general(left, right, (((1,), (1,)), ((), ())), preferred_element_...  18.8 us
  transfers between devices with their start and end apart: 8, of which 7 were waited for; matrix products, arithmetic and copies ran while one was open for 34% of the time, Pallas kernels for 0%

commit v1 on v0

--- a/solution.py
+++ b/solution.py
@@ -6,6 +6,13 @@
 
 BLOCK = 64
 HEAD_DIM = 128
+
+
+def exchange_gather(array, name, dim):
+    n_dev = lax.axis_size(name)
+    blocks = jnp.stack([array for _ in range(n_dev)])
+    blocks = lax.all_to_all(blocks, name, split_axis=0, concat_axis=0)
+    return jnp.concatenate(blocks, axis=dim)
 
 
 def expand(weight, mask):
@@ -56,7 +63,7 @@
     out_heads = output_rows.reshape(
         col_share, output_rows.shape[1] // HEAD_DIM, HEAD_DIM
     ).transpose(1, 0, 2)
-    cot_all = lax.all_gather(grad_out, "col", axis=0, tiled=True)
+    cot_all = exchange_gather(grad_out, "col", 0)
     piece = cot_all
     grad_hidden = lax.psum_scatter(
         times_transposed(piece, w_down).astype(jnp.bfloat16), "row", scatter_dimension=0, tiled=True

time: 491 us -> 404 us (0.82)
  waiting for transfers between devices: 305 us -> 199 us
  starting transfers between devices: 0.72 us -> 7.84 us
  local copies, waits for them, and re-layouts: 102 us -> 109 us
    reduce_scatter x1, waiting for transfers between devices: 72.4 us -> 19.2 us  [body(): lax.psum_scatter(times_transposed(piece, w_up).astype(jnp.bfloat16), 'col...]
    all_gather x1 -> x0, waiting for transfers between devices: 35.9 us -> none  [body(): cot_all = lax.all_gather(grad_out, 'col', axis=0, tiled=True)]
    unnamed x10 -> x9, waiting for transfers between devices: 86 us -> 53 us
    all_to_all x0 -> x1, waiting for transfers between devices: none -> 24.5 us  [exchange_gather(): blocks = lax.all_to_all(blocks, name, split_axis=0, concat_axis=0)]
    all_gather x1, waiting for transfers between devices: 13.4 us -> 0.01 us  [body(): tok_all = lax.all_gather(tokens, 'col', axis=0, tiled=True)]
    all_to_all x0 -> x1, starting transfers between devices: none -> 7.15 us  [exchange_gather(): blocks = lax.all_to_all(blocks, name, split_axis=0, concat_axis=0)]
    all_gather x1, waiting for transfers between devices: 45 us -> 50.7 us  [body(): grad_pre_all = lax.all_gather(grad_pre, 'row', axis=0, tiled=True)]
  transfers between devices with their start and end apart: 8 -> 8, of which waited for: 7 -> 6; matrix products, arithmetic and copies ran while one was open for 34% -> 44% of each run, Pallas kernels for 0% -> 0%
where the time goes in v1:
time: 404 us; the launch traced here: 402 us
  waiting for transfers between devices  199 us (49%)
  local copies, waits for them, and re-layouts  109 us (27%)
  matrix products  60.8 us (15%)
  between operations  15.5 us (4%)
  other arithmetic  10.5 us (3%)
  starting transfers between devices  7.84 us (2%)
    mul x8, local copies, waits for them, and re-layouts, expand(): tiles = tiles * mask.astype(weight.dtype)[:, None, :, None]  84.6 us
    unnamed x9, waiting for transfers between devices  53 us
    all_gather x1, waiting for transfers between devices, body(): hidden_all = lax.all_gather(hidden, 'row', axis=0, tiled=True)  51.8 us
    all_gather x1, waiting for transfers between devices, body(): grad_pre_all = lax.all_gather(grad_pre, 'row', axis=0, tiled=True)  50.7 us
    all_to_all x1, waiting for transfers between devices, exchange_gather(): blocks = lax.all_to_all(blocks, name, split_axis=0, concat_axis=0)  24.5 us
    dot_general x2, matrix products, over_tokens(): lax.dot_general(left, right, (((0,), (0,)), ((), ())), preferred_element_...  20.5 us
    dot_general x2, matrix products, times_transposed(): lax.dot_general(left, right, (((1,), (1,)), ((), ())), preferred_element_...  20.1 us
    unnamed x12, local copies, waits for them, and re-layouts  19.8 us
  transfers between devices with their start and end apart: 8, of which 6 were waited for; matrix products, arithmetic and copies ran while one was open for 44% of the time, Pallas kernels for 0%

profile of v1, /device:TPU:0, one launch (start us, length us, event | category | flops | bytes accessed | tf_op | source)
XLA Modules:
  0.0 402.4 jit_solution(2354749235322496909)
XLA Ops:
  8.0 0.0 all-gather.4.cloned.1.call-start
  8.0 0.7 all-gather.4.cloned.1.call-update
  8.7 0.0 copy-start.1
  8.7 2.9 stack.2
  11.6 7.1 %all-to-all-start = ((bf16[16,64,1536]{2,1,0:T(8,128)(2,1)}), bf16[16,64,1536]{2,1,0:T(8,128)(2,1)S(1)}, u32[]{:S(2)}, u32[]{:S(2)}) async-start(bf16[16,64,1536]{2,1,0:T(8,128)(2,1)} %stack.2), calls=%async_computation.1 | async-start | bytes 6291456 | tf_op jit(solution)/shard_map/all_to_all | solution.py:14
  18.8 0.0 reduce-scatter.15.cloned.1.call-start
  18.8 0.0 copy-done.1
  18.9 4.9 %mul.107 = bf16[24,64,24,64]{3,2,1,0:T(8,128)(2,1)} broadcast(bf16[24,24]{1,0:T(8,128)(2,1)S(1)} %get-tuple-element.19), dimensions={0,2} | broadcast | bytes 4719744 | tf_op jit(solution)/shard_map/mul | solution.py:21
  23.8 13.1 %mul.108 = bf16[1536,1536]{1,0:T(8,128)(2,1)} reshape(bf16[24,64,24,64]{3,2,1,0:T(8,128)(2,1)} %mul.107) | data formatting | bytes 9437184 | tf_op jit(solution)/shard_map/mul | solution.py:21
  36.9 24.5 %all-to-all-done = bf16[16,64,1536]{2,1,0:T(8,128)(2,1)S(1)} async-done(((bf16[16,64,1536]{2,1,0:T(8,128)(2,1)}), bf16[16,64,1536]{2,1,0:T(8,128)(2,1)S(1)}, u32[]{:S(2)}, u32[]{:S(2)}) %all-to-all-start) | async-done | bytes 3145760 | tf_op jit(solution)/shard_map/all_to_all | solution.py:14
  61.4 10.6 %fusion.4 = bf16[1024,1536]{0,1:T(8,128)(2,1)} fusion(bf16[1024,1536]{1,0:T(8,128)(2,1)S(1)} %bitcast.32, bf16[1536,1536]{1,0:T(8,128)(2,1)} %param.9, bf16[1536,1536]{1,0:T(8,128)(2,1)} %mul.108), kind=kOutput, calls=%fused_computation.11 | convolution fusion | flops 4835770368 | bytes 15728640 | tf_op jit(solution)/shard_map/dot_general | solution.py:30
  72.0 0.0 copy-start.2
  72.0 4.7 %copy.21 = bf16[1024,1536]{1,0:T(8,128)(2,1)} copy(bf16[1024,1536]{0,1:T(8,128)(2,1)} %fusion.4) | data formatting | bytes 6291456
  76.7 0.0 reduce-scatter.15.cloned.1.call-update
  76.7 0.2 reduce-scatter.13.cloned.1.call-start
  76.9 0.0 copy-done.2
  76.9 0.6 fusion.19
  77.5 4.9 %mul.100 = bf16[24,64,24,64]{3,2,1,0:T(8,128)(2,1)} broadcast(bf16[24,24]{1,0:T(8,128)(2,1)S(1)} %get-tuple-element.21), dimensions={0,2} | broadcast | bytes 4719744 | tf_op jit(solution)/shard_map/mul | solution.py:21
  82.5 13.1 %mul.101 = bf16[1536,1536]{1,0:T(8,128)(2,1)} reshape(bf16[24,64,24,64]{3,2,1,0:T(8,128)(2,1)} %mul.100) | data formatting | bytes 9437184 | tf_op jit(solution)/shard_map/mul | solution.py:21
  95.5 7.3 %mul.102 = bf16[1536,1536]{1,0:T(8,128)(2,1)} multiply(bf16[1536,1536]{1,0:T(8,128)(2,1)} %param.7, bf16[1536,1536]{1,0:T(8,128)(2,1)} %mul.101) | non-fusion elementwise | flops 2359296 | bytes 14155776 | tf_op jit(solution)/shard_map/mul | solution.py:21
  102.9 0.0 all-gather.4.cloned.1.call-done
  102.9 9.5 %fusion.3 = bf16[1024,1536]{0,1:T(8,128)(2,1)} fusion(bf16[1536,1536]{1,0:T(8,128)(2,1)} %mul.102, bf16[1024,1536]{1,0:T(8,128)(2,1)} %all-gather.4.cloned.1.call-done), kind=kOutput, calls=%fused_computation.10 | convolution fusion | flops 4833411072 | bytes 11010048 | tf_op jit(solution)/shard_map/dot_general | solution.py:49
  112.4 4.7 %copy.19 = bf16[1024,1536]{1,0:T(8,128)(2,1)} copy(bf16[1024,1536]{0,1:T(8,128)(2,1)} %fusion.3) | data formatting | bytes 6291456
  117.1 0.0 reduce-scatter.13.cloned.1.call-update
  117.1 0.0 all-gather.6.cloned.1.call-start
  117.2 4.5 %reduce-scatter.15.cloned.1.call-done = bf16[128,1536]{1,0:T(8,128)(2,1)} async-done(((bf16[1024,1536]{1,0:T(8,128)(2,1)}), bf16[128,1536]{1,0:T(8,128)(2,1)}) %reduce-scatter.15.cloned.1.call-update) | async-done | bytes 393232
  121.6 1.2 copy.22
  122.9 47.0 %reduce-scatter.13.cloned.1.call-done = bf16[128,1536]{1,0:T(8,128)(2,1)} async-done(((bf16[1024,1536]{1,0:T(8,128)(2,1)}), bf16[128,1536]{1,0:T(8,128)(2,1)}) %reduce-scatter.13.cloned.1.call-update) | async-done | bytes 393232
  169.9 1.9 copy.20
  171.8 2.6 fusion.10
  174.4 0.0 all-gather.6.cloned.1.call-update
  174.4 0.0 all-gather.8.cloned.1.call-start
  174.5 0.7 all-gather.8.cloned.1.call-update
  175.2 0.0 reduce-scatter.9.cloned.1.call-start
  175.2 51.8 %all-gather.6.cloned.1.call-done = bf16[1024,1536]{0,1:T(8,128)(2,1)} async-done(((bf16[128,1536]{0,1:T(8,128)(2,1)}), bf16[1024,1536]{0,1:T(8,128)(2,1)}) %all-gather.6.cloned.1.call-update) | async-done | bytes 3145744 | tf_op jit(solution)/shard_map/all_gather | solution.py:55
  227.0 10.7 %convolution_convert_fusion.2 = bf16[1024,1536]{1,0:T(8,128)(2,1)} fusion(bf16[1024,1536]{0,1:T(8,128)(2,1)} %all-gather.6.cloned.1.call-done, bf16[1536,1536]{1,0:T(8,128)(2,1)} %param.9, bf16[1536,1536]{1,0:T(8,128)(2,1)} %mul.108), kind=kOutput, calls=%fused_computation.8 | convolution fusion | flops 4835770368 | bytes 15728640 | tf_op jit(solution)/shard_map/dot_general | solution.py:58
  237.6 0.0 reduce-scatter.9.cloned.1.call-update
  237.7 0.0 copy-start
  237.7 0.3 reduce-scatter.11.cloned.1.call-start
  238.0 50.7 %all-gather.8.cloned.1.call-done = bf16[1024,1536]{0,1:T(8,128)(2,1)} async-done(((bf16[128,1536]{0,1:T(8,128)(2,1)}), bf16[1024,1536]{0,1:T(8,128)(2,1)}) %all-gather.8.cloned.1.call-update) | async-done | bytes 3145744 | tf_op jit(solution)/shard_map/all_gather | solution.py:73
  288.7 9.4 %convolution_convert_fusion = bf16[1024,1536]{1,0:T(8,128)(2,1)} fusion(bf16[1024,1536]{0,1:T(8,128)(2,1)} %all-gather.8.cloned.1.call-done, bf16[1536,1536]{1,0:T(8,128)(2,1)} %mul.102), kind=kOutput, calls=%fused_computation.6 | convolution fusion | flops 4833411072 | bytes 11010048 | tf_op jit(solution)/shard_map/dot_general | solution.py:30
  298.1 0.0 reduce-scatter.11.cloned.1.call-update
  298.1 0.0 copy-done
  298.1 0.1 copy.16
  298.2 7.8 %mul.127 = f32[24,64,24,64]{3,2,1,0:T(8,128)} broadcast(f32[24,24]{1,0:T(8,128)S(1)} %get-tuple-element.18), dimensions={0,2} | broadcast | bytes 9439488 | tf_op jit(solution)/shard_map/mul | solution.py:21
  306.0 16.3 %mul.128 = f32[1536,1536]{1,0:T(8,128)} reshape(f32[24,64,24,64]{3,2,1,0:T(8,128)} %mul.127) | data formatting | bytes 18874368 | tf_op jit(solution)/shard_map/mul | solution.py:21
  322.3 7.9 %mul.123 = f32[24,64,24,64]{1,0,3,2:T(8,128)} broadcast(f32[24,24]{0,1:T(8,128)S(1)} %copy.16), dimensions={0,2} | broadcast | bytes 9439488 | tf_op jit(solution)/shard_map/mul | solution.py:21
  330.2 16.6 %mul.124 = f32[1536,1536]{0,1:T(8,128)} reshape(f32[24,64,24,64]{1,0,3,2:T(8,128)} %mul.123) | data formatting | bytes 18874368 | tf_op jit(solution)/shard_map/mul | solution.py:21
  346.9 10.4 %fusion.1 = bf16[1536,1536]{0,1:T(8,128)(2,1)} fusion(f32[1536,1536]{0,1:T(8,128)} %mul.124, bf16[1024,1536]{0,1:T(8,128)(2,1)} %all-gather.8.cloned.1.call-done, bf16[1024,1536]{1,0:T(8,128)(2,1)} %all-gather.4.cloned.1.call-done), kind=kOutput, calls=%fused_computation.4 | convolution fusion | flops 4838916096 | bytes 20447232 | tf_op jit(solution)/shard_map/dot_general | solution.py:36
  357.3 6.6 %copy.18 = bf16[1536,1536]{1,0:T(8,128)(2,1)} copy(bf16[1536,1536]{0,1:T(8,128)(2,1)} %fusion.1) | data formatting | bytes 9437184
  363.9 10.1 %fusion.2 = bf16[1536,1536]{1,0:T(8,128)(2,1)} fusion(f32[1536,1536]{1,0:T(8,128)} %mul.128, bf16[1024,1536]{0,1:T(8,128)(2,1)} %all-gather.6.cloned.1.call-done, bf16[1024,1536]{1,0:T(8,128)(2,1)S(1)} %bitcast.33), kind=kOutput, calls=%fused_computation.5 | convolution fusion | flops 4838916096 | bytes 20447232 | tf_op jit(solution)/shard_map/dot_general | solution.py:36
  374.0 0.0 reduce-scatter.9.cloned.1.call-done
  374.0 1.1 reshape.32
  375.1 0.7 copy.17
  375.8 19.2 %reduce-scatter.11.cloned.1.call-done = bf16[64,1536]{1,0:T(8,128)(2,1)} async-done(((bf16[1024,1536]{1,0:T(8,128)(2,1)}), bf16[64,1536]{1,0:T(8,128)(2,1)}) %reduce-scatter.11.cloned.1.call-update) | async-done | bytes 196624 | tf_op jit(solution)/shard_map/reduce_scatter | solution.py:80
  (1 shorter events, 0.0 us)
Async XLA Ops:
  8.0 94.9 %all-gather.4.cloned.1.call-start = ((), (), s32[]{:S(2)}) async-start(), calls=%async_computation.5 | async-start | bytes 3342336 | tf_op jit(solution)/shard_map/all_gather | solution.py:44
  8.7 10.1 %copy-start.1 = (s32[24,24]{1,0:T(8,128)S(1)}, s32[24,24]{1,0:T(8,128)}, u32[]{:S(2)}) copy-start(s32[24,24]{1,0:T(8,128)} %param.10) | copy-start | bytes 6916
  11.6 49.7 %all-to-all-start = ((bf16[16,64,1536]{2,1,0:T(8,128)(2,1)}), bf16[16,64,1536]{2,1,0:T(8,128)(2,1)S(1)}, u32[]{:S(2)}, u32[]{:S(2)}) async-start(bf16[16,64,1536]{2,1,0:T(8,128)(2,1)} %stack.2), calls=%async_computation.1 | async-start | bytes 6291456 | tf_op jit(solution)/shard_map/all_to_all | solution.py:14
  18.8 102.9 %reduce-scatter.15.cloned.1.call-start = ((), (), s32[]{:S(2)}) async-start(), calls=%async_computation.11 | async-start | bytes 3538944
  72.0 4.9 %copy-start.2 = (s32[24,24]{1,0:T(8,128)S(1)}, s32[24,24]{1,0:T(8,128)}, u32[]{:S(2)}) copy-start(s32[24,24]{1,0:T(8,128)} %param.8) | copy-start | bytes 6916
  76.7 93.2 %reduce-scatter.13.cloned.1.call-start = ((), (), s32[]{:S(2)}) async-start(), calls=%async_computation.10 | async-start | bytes 3538944
  117.1 109.8 %all-gather.6.cloned.1.call-start = ((), (), s32[]{:S(2)}) async-start(), calls=%async_computation.6 | async-start | bytes 3538944 | tf_op jit(solution)/shard_map/all_gather | solution.py:55
  174.4 114.2 %all-gather.8.cloned.1.call-start = ((), (), s32[]{:S(2)}) async-start(), calls=%async_computation.8 | async-start | bytes 3538944 | tf_op jit(solution)/shard_map/all_gather | solution.py:73
  175.2 198.9 %reduce-scatter.9.cloned.1.call-start = ((), (), s32[]{:S(2)}) async-start(), calls=%async_computation.7 | async-start | bytes 3342336 | tf_op jit(solution)/shard_map/reduce_scatter | solution.py:57
  237.7 60.5 %copy-start = (f32[24,24]{1,0:T(8,128)S(1)}, f32[24,24]{1,0:T(8,128)}, u32[]{:S(2)}) copy-start(f32[24,24]{1,0:T(8,128)} %get-tuple-element.20) | copy-start | bytes 6916
  237.7 157.3 %reduce-scatter.11.cloned.1.call-start = ((), (), s32[]{:S(2)}) async-start(), calls=%async_computation.9 | async-start | bytes 3342336 | tf_op jit(solution)/shard_map/reduce_scatter | solution.py:80
Sparse Core Ops, SparseCore 0:
  11.3 72.6 all-gather.3
  237.8 78.2 reduce-scatter.8
  320.8 74.1 reduce-scatter.10
Sparse Core Ops, SparseCore 1:
  76.8 44.8 reduce-scatter.14
  123.9 45.9 reduce-scatter.12
  174.5 52.4 all-gather.5
  228.5 60.0 all-gather.7
